TPU v7x, 128 devices: a whole 4x4x4 slice. The times are simulated.
128 devices in a mesh: row: 8 (over x_hi, y), col: 16 (over z, x_lo, core).
Axes of the slice: x: 4 (x_hi: 2, x_lo: 2; x = x_hi * 2 + x_lo), y: 4, z: 4, core: 2. Of those that a mesh axis runs over, the one named last changes fastest.
Arguments:
- doubles: float32 [32, 32, 192, 192], P(None, None, 'row', 'col'), may hold values from -6 to 6
- cycle_inter: float32 [6144, 6144], P('row', 'col'), may hold values from -0.078125 to 0.078125
Outputs:
- cycle_term: float32 [6144, 6144], P('row', 'col')
All inputs are finite; a program needn't handle non-finite values.
Results may differ from a plain program's by a relative error of at most 0.00007.
Values sent between devices are 32-bit elements; how exact they have to be, the bound alone decides.
A program may use at most 192 MiB of HBM per device.

v0:
```python
import jax
import jax.numpy as jnp
from jax import lax
from jax.sharding import PartitionSpec as P

V = 192


def body(doubles, cycle_inter):
    moved = lax.all_to_all(
        lax.all_to_all(doubles, "row", split_axis=0, concat_axis=2, tiled=True),
        "col",
        split_axis=1,
        concat_axis=3,
        tiled=True,
    )
    kloc = moved.shape[0]
    jloc = moved.shape[1]
    local_panel = jnp.transpose(moved, (0, 2, 1, 3)).reshape(kloc * V, jloc * V)
    amp_panel = lax.all_gather(local_panel, "row", axis=0, tiled=True)
    return jnp.dot(
        lax.all_gather(cycle_inter, "col", axis=1, tiled=True),
        amp_panel,
        precision=lax.Precision.HIGHEST,
        preferred_element_type=jnp.float32,
    )


def solution(mesh):
    placed = (P(None, None, "row", "col"), P("row", "col"))
    return jax.shard_map(
        body, mesh=mesh, in_specs=placed, out_specs=P("row", "col"), check_vma=False
    )
```

profile of v0, /device:TPU:2, one launch (start us, length us, event | category | flops | bytes accessed | tf_op | source)
XLA Modules:
  0.0 340.6 jit_solution(5271880841259820000)
XLA Ops:
  6.5 0.0 all-gather.5.cloned.1.call-start
  6.5 4.2 %reshape.4 = f32[8,1,36864]{2,1,0:T(1,128)S(1)} reshape(f32[32,12,24,32]{3,2,1,0:T(8,128)} %bitcast.20) | data formatting | bytes 2359296
  10.7 24.6 %all_to_all.36 = f32[8,1,36864]{2,1,0:T(1,128)S(1)} all-to-all(f32[8,1,36864]{2,1,0:T(1,128)S(1)} %reshape.4), channel_id=1, replica_groups=mesh['row'=8,'col'=16] {'row'}, dimensions={0} | all-to-all | bytes 2359296 | tf_op jit(solution)/shard_map/all_to_all | solution.py:11
  35.3 0.5 broadcast
  35.8 3.4 %reduce = f32[8,36864]{1,0:T(8,128)S(1)} reduce(f32[8,1,36864]{2,1,0:T(1,128)S(1)} %all_to_all.36, f32[]{:T(128)} %broadcast), dimensions={1}, to_apply=%all_to_all.26.reduce_sub_computation | reduce | bytes 2359300 | tf_op jit(solution)/shard_map/all_to_all | solution.py:11
  39.3 3.8 %reshape.5 = f32[32,12,24,32]{3,2,1,0:T(8,128)} reshape(f32[8,36864]{1,0:T(8,128)S(1)} %reduce) | data formatting | bytes 2359296
  43.0 6.3 %copy.10 = f32[8,4,32,24,12]{3,0,2,4,1:T(8,128)} copy(f32[8,4,32,24,12]{2,3,4,1,0:T(8,128)} %bitcast.17) | data formatting | bytes 2359296 | tf_op jit(solution)/shard_map/all_to_all | solution.py:11
  49.3 4.2 %all_to_all.29 = f32[4,32,192,12]{2,1,3,0:T(8,128)S(1)} reshape(f32[4,32,8,24,12]{3,2,1,4,0:T(8,128)} %bitcast.16) | data formatting | bytes 2359296 | tf_op jit(solution)/shard_map/all_to_all | solution.py:11
  53.5 1.0 copy.11
  54.6 27.5 %all_to_all.37 = f32[4,32,192,12]{2,0,3,1:T(4,128)S(1)} all-to-all(f32[4,32,192,12]{2,0,3,1:T(4,128)S(1)} %copy.11), channel_id=1, replica_groups=mesh['row'=8,'col'=16] {'col'}, dimensions={1} | all-to-all | bytes 2359296 | tf_op jit(solution)/shard_map/all_to_all | solution.py:10
  82.1 1.2 copy.12
  83.3 1.0 copy.13
  84.3 2.3 reshape.3
  86.6 0.0 all-gather.5.cloned.1.call-update
  86.6 0.2 all-gather.3.cloned.1.call-start
  86.8 0.5 all-gather.3.cloned.1.call-update
  87.3 110.6 %all-gather.5.cloned.1.call-done = f32[6144,384]{1,0:T(8,128)} async-done(((f32[768,384]{1,0:T(8,128)}), f32[6144,384]{1,0:T(8,128)}) %all-gather.5.cloned.1.call-update) | async-done | bytes 9437200 | tf_op jit(solution)/shard_map/all_gather | solution.py:20
  197.9 101.8 %all-gather.3.cloned.1.call-done = f32[768,6144]{1,0:T(8,128)} async-done(((f32[768,384]{1,0:T(8,128)}), f32[768,6144]{1,0:T(8,128)}) %all-gather.3.cloned.1.call-update) | async-done | bytes 18874384 | tf_op jit(solution)/shard_map/all_gather | solution.py:22
  299.7 34.1 %fusion = f32[768,384]{1,0:T(8,128)} fusion(f32[768,6144]{1,0:T(8,128)} %all-gather.3.cloned.1.call-done, f32[6144,384]{1,0:T(8,128)} %all-gather.5.cloned.1.call-done), kind=kOutput, calls=%fused_computation | convolution fusion | flops 21743271936 | bytes 29491200 | tf_op jit(solution)/shard_map/dot_general | solution.py:21
Async XLA Ops:
  6.5 191.4 %all-gather.5.cloned.1.call-start = ((), (), s32[]{:S(2)}) async-start(), calls=%async_computation.3 | async-start | bytes 10616832 | tf_op jit(solution)/shard_map/all_gather | solution.py:20
  86.6 213.1 %all-gather.3.cloned.1.call-start = ((), (), s32[]{:S(2)}) async-start(), calls=%async_computation.2 | async-start | bytes 20054016 | tf_op jit(solution)/shard_map/all_gather | solution.py:22
Sparse Core Ops, SparseCore 0:
  86.7 111.1 all-gather.4
  199.6 100.0 all-gather.2
where the time goes:
time: 342 us; the launch traced here: 341 us
  waiting for transfers between devices  213 us (62%)
  blocking collectives  52.1 us (15%)
  matrix products  34.1 us (10%)
  local copies, waits for them, and re-layouts  24.5 us (7%)
  between operations  13.4 us (4%)
  other arithmetic  3.45 us (1%)
    all_gather x1, waiting for transfers between devices, body(): amp_panel = lax.all_gather(local_panel, 'row', axis=0, tiled=True)  111 us
    all_gather x1, waiting for transfers between devices, body(): lax.all_gather(cycle_inter, 'col', axis=1, tiled=True)  102 us
    dot_general x1, matrix products, body(): jnp.dot(lax.all_gather(cycle_inter, 'col', axis=1, tiled=True), amp_panel...  34.1 us
    all_to_all x1, blocking collectives, body(): lax.all_to_all(lax.all_to_all(doubles, 'row', split_axis=0, concat_axis=2...  27.5 us
    all_to_all x1, blocking collectives, body(): lax.all_to_all(doubles, 'row', split_axis=0, concat_axis=2, tiled=True)  24.6 us
    all_to_all x4, local copies, waits for them, and re-layouts, body(): lax.all_to_all(doubles, 'row', split_axis=0, concat_axis=2, tiled=True)  12 us
    unnamed x2, local copies, waits for them, and re-layouts  7.95 us
  transfers between devices with their start and end apart: 2, of which 2 were waited for; matrix products, arithmetic and copies ran while one was open for 0% of the time, Pallas kernels for 0%

commit v1 on v0

v1 whole, which is shorter than its diff:
```python
import functools

import jax
import jax.numpy as jnp
import numpy as np
from jax import lax
from jax.experimental import pallas as pl
from jax.experimental.pallas import tpu as pltpu
from jax.sharding import PartitionSpec as P

MESH = pl.DeviceIdType.MESH
F32, BF16 = jnp.float32, jnp.bfloat16


def permutations():
    pack = np.zeros((2, 192, 384), np.float32)
    for half in range(2):
        for z in range(4):
            for core in range(2):
                for j2 in range(2):
                    for b in range(12):
                        j = 8 * z + 4 * half + 2 * core + j2
                        pack[half, ((z * 2 + core) * 2 + j2) * 12 + b, b * 32 + j] = 1
    unpack = np.zeros((384, 384), np.float32)
    for q in range(16):
        for j2 in range(2):
            for b in range(12):
                unpack[(q * 2 + j2) * 12 + b, j2 * 192 + q * 12 + b] = 1
    return pack, unpack


def halves(x):
    hi = x.astype(BF16)
    return hi, (x - hi.astype(F32)).astype(BF16)


def kernel(
    d_hbm, w_hbm, pack_hbm, unpack_hbm, out_ref,
    d, pack, unpack, x, t, r, amp, wb, whi, wlo, ahi, alo, acc, part,
    in_sem, a2a_s, a2a_r, x_s, x_r, y_s, y_r, f_s, f_r,
    w_s, w_r, g_s, g_r, n_s, n_r, c_s, c_r,
):
    row, col = lax.axis_index("row"), lax.axis_index("col")
    xh, y = row // 4, row % 4
    z, xl, core = col // 4, (col // 2) % 2, col % 2

    def dev(xh_, y_, z_, xl_, core_):
        return (xh_ * 4 + y_, z_ * 4 + xl_ * 2 + core_)

    ynext = (dev(xh, (y + 1) % 4, z, xl, core), dev(xh, (y + 3) % 4, z, xl, core))
    znext = (dev(xh, y, (z + 1) % 4, xl, core), dev(xh, y, (z + 3) % 4, xl, core))
    other_xh = dev(1 - xh, y, z, xl, core)
    other_xl = dev(xh, y, z, 1 - xl, core)
    twin = dev(xh, y, z, xl, 1 - core)

    loads = [
        pltpu.make_async_copy(d_hbm, d, in_sem.at[0]),
        pltpu.make_async_copy(pack_hbm, pack, in_sem.at[1]),
        pltpu.make_async_copy(unpack_hbm, unpack, in_sem.at[2]),
        pltpu.make_async_copy(w_hbm, wb.at[z, core], in_sem.at[3]),
    ]
    for load in loads:
        load.start()

    barrier = pltpu.get_barrier_semaphore()

    def greet(o, _):
        pl.semaphore_signal(barrier, inc=1, device_id=(row, (col + o) % 16), device_id_type=MESH)
        return 0

    lax.fori_loop(1, 16, greet, 0)
    for peer in ynext + (other_xh,):
        pl.semaphore_signal(barrier, inc=1, device_id=peer, device_id_type=MESH)
    pl.semaphore_wait(barrier, 18)

    def remote(src, dst, send, recv, to):
        return pltpu.make_async_remote_copy(
            src_ref=src, dst_ref=dst, send_sem=send, recv_sem=recv, device_id=to, device_id_type=MESH
        )

    def w_own(way, quarter):
        rows = pl.ds(quarter * 192, 192)
        return remote(w_hbm.at[rows], wb.at[z, core, rows], w_s.at[way, quarter], w_r.at[way, quarter], znext[way])

    def w_came(way, quarter):
        at = (z + 3) % 4 if way == 0 else (z + 1) % 4
        rows = pl.ds(quarter * 192, 192)
        return remote(wb.at[at, core, rows], wb.at[at, core, rows], w_s.at[way, quarter], w_r.at[way, quarter], znext[way])

    def w_pass(way):
        at = (z + 3) % 4 if way == 0 else (z + 1) % 4
        rows = pl.ds(way * 384, 384)
        return remote(wb.at[at, core, rows], wb.at[at, core, rows], g_s.at[way], g_r.at[way], znext[way])

    def w_passed(way):
        at = (z + 2) % 4
        rows = pl.ds(way * 384, 384)
        return remote(wb.at[at, core, rows], wb.at[at, core, rows], g_s.at[way], g_r.at[way], znext[way])

    def w_twin(off):
        at = (z + off) % 4
        src = w_hbm if off == 0 else wb.at[at, core]
        return remote(src, wb.at[at, core], n_s.at[off], n_r.at[off], twin)

    def w_twin_came(off):
        at = (z + off) % 4
        return remote(wb.at[at, 1 - core], wb.at[at, 1 - core], n_s.at[off], n_r.at[off], twin)

    def a2a(h, o):
        to = (col + o) % 16
        txl = (to // 2) % 2
        tz = (to // 4) * 2 + to % 2
        return remote(
            t.at[txl, (txl + 1 + h) % 2, tz], r.at[h, col], a2a_s.at[h, to], a2a_r.at[h, col], (row, to)
        )

    def a2a_came(h, o):
        src = (col + o) % 16
        return remote(r.at[h, src], r.at[h, src], a2a_s.at[h, src], a2a_r.at[h, src], (row, src))

    def send_a2a(h):
        def go(o, _):
            a2a(h, o).start()
            return 0

        lax.fori_loop(1, 16, go, 0)
        r[h, col] = t[xl, (xl + 1 + h) % 2, z * 2 + core]

    def unpack_half(h):
        def wait(o, _):
            a2a_came(h, o).wait_recv()
            return 0

        lax.fori_loop(1, 16, wait, 0)
        hi, lo = halves(jnp.transpose(r[h].reshape(384, 384)))
        block = jnp.dot(hi, unpack[...], preferred_element_type=F32)
        block += jnp.dot(lo, unpack[...], preferred_element_type=F32)
        amp[h, :, row] = block.reshape(16, 24, 384)

    def pack_half(lanes, half):
        hi, lo = halves(x[lanes].reshape(384, 384))
        nt = (((1,), (1,)), ((), ()))
        rows = lax.dot_general(pack[half], hi, nt, preferred_element_type=F32)
        rows += lax.dot_general(pack[half], lo, nt, preferred_element_type=F32)
        t[lanes, half] = rows.reshape(8, 24, 384)

    def place(s):
        p = s % 4
        return s // 4, (z + p + p // 2 - 2 * (p // 3)) % 4

    def slab(s, at, first=0, count=4):
        h, zz = place(s)
        return amp.at[h, pl.ds(zz * 4 + first, count), at]

    far = (1 - xh) * 4 + y

    def x_send(s):
        return remote(slab(s, row), slab(s, row), x_s.at[s], x_r.at[s], other_xh)

    def x_came(s):
        return remote(slab(s, far), slab(s, far), x_s.at[s], x_r.at[s], other_xh)

    def y_send(s, way, which):
        at = far if which else row
        return remote(slab(s, at), slab(s, at), y_s.at[s, way, which], y_r.at[s, way, which], ynext[way])

    def y_row(way, which, steps):
        at_xh = 1 - xh if which else xh
        return at_xh * 4 + (y + (4 - steps if way == 0 else steps)) % 4

    def y_came(s, way, which):
        at = y_row(way, which, 1)
        return remote(slab(s, at), slab(s, at), y_s.at[s, way, which], y_r.at[s, way, which], ynext[way])

    def f_send(s, way, which):
        at = y_row(way, which, 1)
        view = slab(s, at, 2 * way, 2)
        return remote(view, view, f_s.at[s, way, which], f_r.at[s, way, which], ynext[way])

    def f_came(s, way, which):
        at = y_row(way, which, 2)
        view = slab(s, at, 2 * way, 2)
        return remote(view, view, f_s.at[s, way, which], f_r.at[s, way, which], ynext[way])

    def split_w(zz):
        def block(m, _):
            rows = pl.ds(pl.multiple_of(m * 128, 128), 128)
            for c in range(2):
                hi, lo = halves(wb[zz, c, rows, :])
                whi[zz, rows, c * 384 : (c + 1) * 384] = hi
                wlo[zz, rows, c * 384 : (c + 1) * 384] = lo
            return 0

        lax.fori_loop(0, 6, block, 0)

    def compute(s):
        h, zz = place(s)

        @pl.when(s < 4)
        def _():
            split_w(zz)

        def split_a(k, _):
            hi, lo = halves(amp[h, zz * 4 + k].reshape(192, 384))
            rows = pl.ds(pl.multiple_of(k * 192, 64), 192)
            ahi[rows, :] = hi
            alo[rows, :] = lo
            return 0

        lax.fori_loop(0, 4, split_a, 0)

        def block(m, _):
            rows = pl.ds(pl.multiple_of(m * 256, 256), 256)
            a_hi, a_lo = ahi[...], alo[...]
            w_hi = whi[zz, rows, :]
            total = jnp.dot(w_hi, a_hi, preferred_element_type=F32)
            total += jnp.dot(w_hi, a_lo, preferred_element_type=F32)
            total += jnp.dot(wlo[zz, rows, :], a_hi, preferred_element_type=F32)
            acc[h, rows, :] += total
            return 0

        lax.fori_loop(0, 3, block, 0)

    def c_send():
        return remote(acc.at[0], part, c_s, c_r, other_xl)

    for way in range(2):
        w_own(way, 0).start()
    w_twin(0).start()
    acc[...] = jnp.zeros_like(acc)
    loads[0].wait()
    for lanes in range(2):
        for quad in range(3):
            for kk in range(16):
                k = 8 * (kk // 4) + 4 * lanes + kk % 4
                x[lanes, kk, :, quad * 128 : (quad + 1) * 128] = jnp.concatenate(
                    [d[k, quad * 4 + i] for i in range(4)], axis=-1
                )
    loads[1].wait()
    pack_half(0, 1)
    pack_half(1, 0)
    send_a2a(0)
    for way in range(2):
        for quarter in range(1, 4):
            w_own(way, quarter).start()
    pack_half(0, 0)
    pack_half(1, 1)
    send_a2a(1)
    loads[2].wait()
    unpack_half(0)

    def each_x(first):
        def go(s, _):
            x_send(s).start()
            return 0

        lax.fori_loop(first, first + 4, go, 0)

    each_x(0)
    for way in range(2):
        y_send(0, way, 0).start()
    x_came(0).wait_recv()
    for way in range(2):
        y_send(0, way, 1).start()
    loads[3].wait()

    def body(s, _):
        @pl.when(s < 7)
        def _():
            for way in range(2):
                y_send(s + 1, way, 0).start()
            x_came(s + 1).wait_recv()
            for way in range(2):
                y_send(s + 1, way, 1).start()

        for which in range(2):
            for way in range(2):
                y_came(s, way, which).wait_recv()
                f_send(s, way, which).start()

        @pl.when(s == 2)
        def _():
            for way in range(2):
                for quarter in range(4):
                    w_came(way, quarter).wait_recv()
                w_pass(way).start()
            w_twin(3).start()
            w_twin(1).start()
            w_twin_came(0).wait_recv()

        @pl.when(s == 3)
        def _():
            w_twin_came(1).wait_recv()
            w_twin_came(3).wait_recv()

        @pl.when(s == 4)
        def _():
            for way in range(2):
                w_passed(way).wait_recv()
            w_twin(2).start()

        @pl.when(s == 5)
        def _():
            w_twin_came(2).wait_recv()

        @pl.when(s >= 2)
        def _():
            compute(s - 2)

        @pl.when(s == 2)
        def _():
            unpack_half(1)
            each_x(4)

        @pl.when(s == 6)
        def _():
            c_send().start()

        @pl.when(s >= 1)
        def _():
            for which in range(2):
                for way in range(2):
                    f_came(s - 1, way, which).wait_recv()

        return 0

    lax.fori_loop(0, 8, body, 0)
    compute(6)
    for which in range(2):
        for way in range(2):
            f_came(7, way, which).wait_recv()
    compute(7)
    c_send().wait_recv()
    out_ref[...] = acc[1] + part[...]

    def drain_a2a(o, _):
        for h in range(2):
            a2a(h, o).wait_send()
        return 0

    lax.fori_loop(1, 16, drain_a2a, 0)

    def drain_y(s, _):
        x_send(s).wait_send()
        for which in range(2):
            for way in range(2):
                y_send(s, way, which).wait_send()
                f_send(s, way, which).wait_send()
        return 0

    lax.fori_loop(0, 8, drain_y, 0)
    for way in range(2):
        for quarter in range(4):
            w_own(way, quarter).wait_send()
        w_pass(way).wait_send()
    for off in range(4):
        w_twin(off).wait_send()
    c_send().wait_send()


def body(doubles, cycle_inter):
    pack, unpack = permutations()
    vmem, sems = pltpu.VMEM, pltpu.SemaphoreType.DMA
    return pl.pallas_call(
        kernel,
        out_shape=jax.ShapeDtypeStruct((768, 384), F32),
        in_specs=[pl.BlockSpec(memory_space=pl.ANY)] * 4,
        out_specs=pl.BlockSpec(memory_space=pltpu.VMEM),
        scratch_shapes=[
            vmem((32, 12, 24, 32), F32),
            vmem((2, 192, 384), BF16),
            vmem((384, 384), BF16),
            vmem((2, 16, 24, 384), F32),
            vmem((2, 2, 8, 24, 384), F32),
            vmem((2, 16, 24, 384), F32),
            vmem((2, 16, 8, 24, 384), F32),
            vmem((4, 2, 768, 384), F32),
            vmem((4, 768, 768), BF16),
            vmem((4, 768, 768), BF16),
            vmem((768, 384), BF16),
            vmem((768, 384), BF16),
            vmem((2, 768, 384), F32),
            vmem((768, 384), F32),
            sems((4,)),
            sems((2, 16)), sems((2, 16)),
            sems((8,)), sems((8,)),
            sems((8, 2, 2)), sems((8, 2, 2)),
            sems((8, 2, 2)), sems((8, 2, 2)),
            sems((2, 4)), sems((2, 4)),
            sems((2,)), sems((2,)),
            sems((4,)), sems((4,)),
            sems, sems,
        ],
        compiler_params=pltpu.CompilerParams(
            collective_id=1, has_side_effects=True, vmem_limit_bytes=62 * 1024 * 1024
        ),
        name="cycle_term",
    )(
        jnp.transpose(doubles, (0, 3, 2, 1)),
        cycle_inter,
        jnp.asarray(pack, BF16),
        jnp.asarray(unpack, BF16),
    )


def solution(mesh):
    return jax.shard_map(
        body,
        mesh=mesh,
        in_specs=(P(None, None, "row", "col"), P("row", "col")),
        out_specs=P("row", "col"),
        check_vma=False,
    )
```

time: 342 us -> 127 us (0.37)
  waiting for transfers between devices: 213 us -> 0 us
  Pallas kernels: 0 us -> 124 us
  blocking collectives: 52.1 us -> 0 us
  matrix products: 34.1 us -> 0 us
  local copies, waits for them, and re-layouts: 24.5 us -> 2.36 us
  between operations: 13.4 us -> 0.01 us
  other arithmetic: 3.45 us -> 0 us
    all_gather x2 -> x0, waiting for transfers between devices: 212 us -> none  [the longest x1 111 us: body(): amp_panel = lax.all_gather(local_panel, 'row', axis=0, tiled=True)]
    pallas_call x0 -> x1, Pallas kernels: none -> 124 us  [body(): pl.pallas_call(kernel, out_shape=jax.ShapeDtypeStruct((768, 384), F32), i...]
    all_to_all x2 -> x0, blocking collectives: 52.1 us -> none  [the longest x1 27.5 us: body(): lax.all_to_all(lax.all_to_all(doubles, 'row', split_axis=0, concat_axis=2...]
    dot_general x1 -> x0, matrix products: 34.1 us -> none  [body(): jnp.dot(lax.all_gather(cycle_inter, 'col', axis=1, tiled=True), amp_panel...]
    all_to_all x5 -> x0, local copies, waits for them, and re-layouts: 13.2 us -> none  [the longest x4 12 us: body(): lax.all_to_all(doubles, 'row', split_axis=0, concat_axis=2, tiled=True)]
    unnamed x2 -> x1, local copies, waits for them, and re-layouts: 7.95 us -> 2.36 us
    all_to_all x1 -> x0, other arithmetic: 3.45 us -> none  [body(): lax.all_to_all(doubles, 'row', split_axis=0, concat_axis=2, tiled=True)]
  transfers between devices with their start and end apart: 2 -> 0, of which waited for: 2 -> 0; matrix products, arithmetic and copies ran while one was open for 0% -> 0% of each run, Pallas kernels for 0% -> 0%
where the time goes in v1:
time: 127 us
  Pallas kernels  124 us (98%)
  local copies, waits for them, and re-layouts  2.36 us (2%)
    pallas_call x1, Pallas kernels, body(): pl.pallas_call(kernel, out_shape=jax.ShapeDtypeStruct((768, 384), F32), i...  124 us

profile of v1, /device:TPU:2, one launch (start us, length us, event | category | flops | bytes accessed | tf_op | source)
XLA Modules:
  0.0 126.7 jit_solution(3613385219280801399)
XLA Ops:
  0.0 124.3 %cycle_term.1 = f32[768,384]{1,0:T(8,128)} custom-call(f32[32,12,24,32]{3,2,1,0:T(8,128)} %bitcast.1, f32[768,384]{1,0:T(8,128)} %w_hbm.1, bf16[2,192,384]{2,1,0:T(8,128)(2,1)} %constant.4.clone.pack_hbm, bf16[384,384]{1,0:T(8,128)(2,1)} %constant.5.clone.unpack_hbm), custom_call_target="tpu_custom_call" | custom-call | tf_op jit(solution)/shard_map/cycle_term/pallas_call | solution.py:364
  124.3 2.4 %copy.6 = f32[768,384]{1,0:T(8,128)} copy(f32[768,384]{1,0:T(8,128)} %cycle_term.1) | data formatting | bytes 2359296

commit v2 on v1

--- a/solution.py
+++ b/solution.py
@@ -312,7 +312,7 @@
             unpack_half(1)
             each_x(4)
 
-        @pl.when(s == 6)
+        @pl.when(s == 5)
         def _():
             c_send().start()
 

time: 127 us -> 118 us (0.929)
  Pallas kernels: 124 us -> 115 us
    pallas_call x1, Pallas kernels: 124 us -> 115 us  [body(): pl.pallas_call(kernel, out_shape=jax.ShapeDtypeStruct((768, 384), F32), i...]
where the time goes in v2:
time: 118 us
  Pallas kernels  115 us (97%)
  local copies, waits for them, and re-layouts  2.36 us (2%)
    pallas_call x1, Pallas kernels, body(): pl.pallas_call(kernel, out_shape=jax.ShapeDtypeStruct((768, 384), F32), i...  115 us
    unnamed x1, local copies, waits for them, and re-layouts  2.36 us

profile of v2, /device:TPU:2, one launch (start us, length us, event | category | flops | bytes accessed | tf_op | source)
XLA Modules:
  0.0 117.6 jit_solution(3764493684553596354)
XLA Ops:
  0.0 115.2 %cycle_term.1 = f32[768,384]{1,0:T(8,128)} custom-call(f32[32,12,24,32]{3,2,1,0:T(8,128)} %bitcast.1, f32[768,384]{1,0:T(8,128)} %w_hbm.1, bf16[2,192,384]{2,1,0:T(8,128)(2,1)} %constant.4.clone.pack_hbm, bf16[384,384]{1,0:T(8,128)(2,1)} %constant.5.clone.unpack_hbm), custom_call_target="tpu_custom_call" | custom-call | tf_op jit(solution)/shard_map/cycle_term/pallas_call | solution.py:364
  115.2 2.4 %copy.6 = f32[768,384]{1,0:T(8,128)} copy(f32[768,384]{1,0:T(8,128)} %cycle_term.1) | data formatting | bytes 2359296

commit v3 on v2

--- a/solution.py
+++ b/solution.py
@@ -53,6 +53,16 @@
     other_xl = dev(xh, y, z, 1 - xl, core)
     twin = dev(xh, y, z, xl, 1 - core)
 
+    barrier = pltpu.get_barrier_semaphore()
+
+    def greet(o, _):
+        pl.semaphore_signal(barrier, inc=1, device_id=(row, (col + o) % 16), device_id_type=MESH)
+        return 0
+
+    lax.fori_loop(1, 16, greet, 0)
+    for peer in ynext + (other_xh,):
+        pl.semaphore_signal(barrier, inc=1, device_id=peer, device_id_type=MESH)
+
     loads = [
         pltpu.make_async_copy(d_hbm, d, in_sem.at[0]),
         pltpu.make_async_copy(pack_hbm, pack, in_sem.at[1]),
@@ -62,30 +72,19 @@
     for load in loads:
         load.start()
 
-    barrier = pltpu.get_barrier_semaphore()
-
-    def greet(o, _):
-        pl.semaphore_signal(barrier, inc=1, device_id=(row, (col + o) % 16), device_id_type=MESH)
-        return 0
-
-    lax.fori_loop(1, 16, greet, 0)
-    for peer in ynext + (other_xh,):
-        pl.semaphore_signal(barrier, inc=1, device_id=peer, device_id_type=MESH)
-    pl.semaphore_wait(barrier, 18)
-
     def remote(src, dst, send, recv, to):
         return pltpu.make_async_remote_copy(
             src_ref=src, dst_ref=dst, send_sem=send, recv_sem=recv, device_id=to, device_id_type=MESH
         )
 
-    def w_own(way, quarter):
-        rows = pl.ds(quarter * 192, 192)
-        return remote(w_hbm.at[rows], wb.at[z, core, rows], w_s.at[way, quarter], w_r.at[way, quarter], znext[way])
-
-    def w_came(way, quarter):
+    def w_own(way, half):
+        rows = pl.ds(half * 384, 384)
+        return remote(w_hbm.at[rows], wb.at[z, core, rows], w_s.at[way, half], w_r.at[way, half], znext[way])
+
+    def w_came(way, half):
         at = (z + 3) % 4 if way == 0 else (z + 1) % 4
-        rows = pl.ds(quarter * 192, 192)
-        return remote(wb.at[at, core, rows], wb.at[at, core, rows], w_s.at[way, quarter], w_r.at[way, quarter], znext[way])
+        rows = pl.ds(half * 384, 384)
+        return remote(wb.at[at, core, rows], wb.at[at, core, rows], w_s.at[way, half], w_r.at[way, half], znext[way])
 
     def w_pass(way):
         at = (z + 3) % 4 if way == 0 else (z + 1) % 4
@@ -224,9 +223,6 @@
     def c_send():
         return remote(acc.at[0], part, c_s, c_r, other_xl)
 
-    for way in range(2):
-        w_own(way, 0).start()
-    w_twin(0).start()
     acc[...] = jnp.zeros_like(acc)
     loads[0].wait()
     for lanes in range(2):
@@ -237,15 +233,18 @@
                     [d[k, quad * 4 + i] for i in range(4)], axis=-1
                 )
     loads[1].wait()
-    pack_half(0, 1)
-    pack_half(1, 0)
+    for half in range(2):
+        pack_half(0, half)
+        pack_half(1, half)
+    pl.semaphore_wait(barrier, 18)
+
     send_a2a(0)
+    w_twin(0).start()
     for way in range(2):
-        for quarter in range(1, 4):
-            w_own(way, quarter).start()
-    pack_half(0, 0)
-    pack_half(1, 1)
+        w_own(way, way).start()
     send_a2a(1)
+    for way in range(2):
+        w_own(way, 1 - way).start()
     loads[2].wait()
     unpack_half(0)
 
@@ -256,45 +255,69 @@
 
         lax.fori_loop(first, first + 4, go, 0)
 
+    def y_part(s):
+        x_came(s).wait_recv()
+        for way in range(2):
+            y_send(s, way, 1).start()
+
+    def y_own(s):
+        for way in range(2):
+            y_send(s, way, 0).start()
+
+    def f_wait(s):
+        for which in range(2):
+            for way in range(2):
+                f_came(s, way, which).wait_recv()
+
     each_x(0)
-    for way in range(2):
-        y_send(0, way, 0).start()
-    x_came(0).wait_recv()
-    for way in range(2):
-        y_send(0, way, 1).start()
+    y_own(0)
+    y_own(1)
+    y_part(0)
     loads[3].wait()
 
     def body(s, _):
+        @pl.when(s == 3)
+        def _():
+            unpack_half(1)
+            each_x(4)
+            y_own(4)
+
         @pl.when(s < 7)
         def _():
-            for way in range(2):
-                y_send(s + 1, way, 0).start()
-            x_came(s + 1).wait_recv()
-            for way in range(2):
-                y_send(s + 1, way, 1).start()
+            y_part(s + 1)
 
         for which in range(2):
             for way in range(2):
                 y_came(s, way, which).wait_recv()
                 f_send(s, way, which).start()
 
+        @pl.when((s < 6) & (s != 2))
+        def _():
+            y_own(s + 2)
+
         @pl.when(s == 2)
         def _():
+            w_twin_came(0).wait_recv()
+
+        @pl.when(s == 3)
+        def _():
             for way in range(2):
-                for quarter in range(4):
-                    w_came(way, quarter).wait_recv()
+                for half in range(2):
+                    w_came(way, half).wait_recv()
                 w_pass(way).start()
             w_twin(3).start()
             w_twin(1).start()
-            w_twin_came(0).wait_recv()
-
-        @pl.when(s == 3)
+
+        @pl.when(s == 4)
         def _():
             w_twin_came(1).wait_recv()
             w_twin_came(3).wait_recv()
 
-        @pl.when(s == 4)
-        def _():
+            def two(n, _):
+                compute(n)
+                return 0
+
+            lax.fori_loop(1, 3, two, 0)
             for way in range(2):
                 w_passed(way).wait_recv()
             w_twin(2).start()
@@ -303,32 +326,23 @@
         def _():
             w_twin_came(2).wait_recv()
 
-        @pl.when(s >= 2)
+        @pl.when((s == 2) | (s >= 5))
         def _():
             compute(s - 2)
 
-        @pl.when(s == 2)
-        def _():
-            unpack_half(1)
-            each_x(4)
-
         @pl.when(s == 5)
         def _():
             c_send().start()
 
         @pl.when(s >= 1)
         def _():
-            for which in range(2):
-                for way in range(2):
-                    f_came(s - 1, way, which).wait_recv()
+            f_wait(s - 1)
 
         return 0
 
     lax.fori_loop(0, 8, body, 0)
     compute(6)
-    for which in range(2):
-        for way in range(2):
-            f_came(7, way, which).wait_recv()
+    f_wait(7)
     compute(7)
     c_send().wait_recv()
     out_ref[...] = acc[1] + part[...]
@@ -350,8 +364,8 @@
 
     lax.fori_loop(0, 8, drain_y, 0)
     for way in range(2):
-        for quarter in range(4):
-            w_own(way, quarter).wait_send()
+        for half in range(2):
+            w_own(way, half).wait_send()
         w_pass(way).wait_send()
     for off in range(4):
         w_twin(off).wait_send()
@@ -386,7 +400,7 @@
             sems((8,)), sems((8,)),
             sems((8, 2, 2)), sems((8, 2, 2)),
             sems((8, 2, 2)), sems((8, 2, 2)),
-            sems((2, 4)), sems((2, 4)),
+            sems((2, 2)), sems((2, 2)),
             sems((2,)), sems((2,)),
             sems((4,)), sems((4,)),
             sems, sems,

time: 118 us -> 110 us (0.932)
  Pallas kernels: 115 us -> 107 us
    pallas_call x1, Pallas kernels: 115 us -> 107 us  [body(): pl.pallas_call(kernel, out_shape=jax.ShapeDtypeStruct((768, 384), F32), i...]
where the time goes in v3:
time: 110 us; the launch traced here: 109 us
  Pallas kernels  107 us (97%)
  local copies, waits for them, and re-layouts  2.36 us (2%)
    pallas_call x1, Pallas kernels, body(): pl.pallas_call(kernel, out_shape=jax.ShapeDtypeStruct((768, 384), F32), i...  107 us
    unnamed x1, local copies, waits for them, and re-layouts  2.36 us

profile of v3, /device:TPU:2, one launch (start us, length us, event | category | flops | bytes accessed | tf_op | source)
XLA Modules:
  0.0 109.3 jit_solution(758659304764091281)
XLA Ops:
  0.0 106.9 %cycle_term.1 = f32[768,384]{1,0:T(8,128)} custom-call(f32[32,12,24,32]{3,2,1,0:T(8,128)} %bitcast.1, f32[768,384]{1,0:T(8,128)} %w_hbm.1, bf16[2,192,384]{2,1,0:T(8,128)(2,1)} %constant.4.clone.pack_hbm, bf16[384,384]{1,0:T(8,128)(2,1)} %constant.5.clone.unpack_hbm), custom_call_target="tpu_custom_call" | custom-call | tf_op jit(solution)/shard_map/cycle_term/pallas_call | solution.py:378
  106.9 2.4 %copy.6 = f32[768,384]{1,0:T(8,128)} copy(f32[768,384]{1,0:T(8,128)} %cycle_term.1) | data formatting | bytes 2359296

commit v4 on v3

v4 whole, which is shorter than its diff:
```python
import functools

import jax
import jax.numpy as jnp
import numpy as np
from jax import lax
from jax.experimental import pallas as pl
from jax.experimental.pallas import tpu as pltpu
from jax.sharding import PartitionSpec as P

MESH = pl.DeviceIdType.MESH
F32, BF16 = jnp.float32, jnp.bfloat16


def permutations():
    pack = np.zeros((2, 192, 384), np.float32)
    for half in range(2):
        for z in range(4):
            for core in range(2):
                for j2 in range(2):
                    for b in range(12):
                        j = 8 * z + 4 * half + 2 * core + j2
                        pack[half, ((z * 2 + core) * 2 + j2) * 12 + b, b * 32 + j] = 1
    unpack = np.zeros((384, 384), np.float32)
    for q in range(16):
        for j2 in range(2):
            for b in range(12):
                unpack[(q * 2 + j2) * 12 + b, j2 * 192 + q * 12 + b] = 1
    return pack, unpack


def halves(x):
    hi = x.astype(BF16)
    return hi, (x - hi.astype(F32)).astype(BF16)


EARLY = 1


def kernel(
    d_hbm, w_hbm, pack_hbm, unpack_hbm, out_ref,
    d, pack, unpack, x, t, r, amp, wb, whi, wlo, ahi, alo, acc, part,
    in_sem, a2a_s, a2a_r, x_s, x_r, e_s, e_r, y_s, y_r, f_s, f_r,
    w_s, w_r, g_s, g_r, n_s, n_r, c_s, c_r,
):
    row, col = lax.axis_index("row"), lax.axis_index("col")
    xh, y = row >> 2, row & 3
    z, xl, core = col >> 2, (col >> 1) & 1, col & 1

    def dev(xh_, y_, z_, xl_, core_):
        return (xh_ * 4 + y_, z_ * 4 + xl_ * 2 + core_)

    ynext = (dev(xh, (y + 1) & 3, z, xl, core), dev(xh, (y + 3) & 3, z, xl, core))
    znext = (dev(xh, y, (z + 1) & 3, xl, core), dev(xh, y, (z + 3) & 3, xl, core))
    zfrom = ((z + 3) & 3, (z + 1) & 3)
    other_xh = dev(1 - xh, y, z, xl, core)
    other_xl = dev(xh, y, z, 1 - xl, core)
    twin = dev(xh, y, z, xl, 1 - core)

    barrier = pltpu.get_barrier_semaphore()

    def greet(o, _):
        pl.semaphore_signal(barrier, inc=1, device_id=(row, (col + o) & 15), device_id_type=MESH)
        return 0

    lax.fori_loop(1, 16, greet, 0)
    for peer in ynext + (other_xh,):
        pl.semaphore_signal(barrier, inc=1, device_id=peer, device_id_type=MESH)

    loads = [
        pltpu.make_async_copy(d_hbm, d, in_sem.at[0]),
        pltpu.make_async_copy(pack_hbm, pack, in_sem.at[1]),
        pltpu.make_async_copy(unpack_hbm, unpack, in_sem.at[2]),
        pltpu.make_async_copy(w_hbm, wb.at[z, core], in_sem.at[3]),
    ]
    for load in loads:
        load.start()

    def remote(src, dst, send, recv, to):
        return pltpu.make_async_remote_copy(
            src_ref=src, dst_ref=dst, send_sem=send, recv_sem=recv, device_id=to, device_id_type=MESH
        )

    W_ROWS = ((0, 384), (384, 192), (576, 192))

    def w_own(way, p):
        rows = pl.ds(*W_ROWS[p])
        return remote(w_hbm.at[rows], wb.at[z, core, rows], w_s.at[way, p], w_r.at[way, p], znext[way])

    def w_came(way, p):
        view = wb.at[zfrom[way], core, pl.ds(*W_ROWS[p])]
        return remote(view, view, w_s.at[way, p], w_r.at[way, p], znext[way])

    def w_pass(way, half, at):
        view = wb.at[at, core, pl.ds(half * 384 + way * 192, 192)]
        return remote(view, view, g_s.at[way, half], g_r.at[way, half], znext[way])

    def w_twin(off, half, plane, whole=False):
        view = wb.at[(z + off) & 3, plane] if whole else wb.at[(z + off) & 3, plane, pl.ds(half * 384, 384)]
        return remote(w_hbm if whole else view, view, n_s.at[off, half], n_r.at[off, half], twin)

    def order(z_, s):
        p = s & 3
        return (z_ + (p ^ (p >> 1))) & 3

    def a2a(s, o):
        to = (col + o) & 15
        txl = (to >> 1) & 1
        src = t.at[txl, (txl + 1 + (s >> 2)) & 1, order(to >> 2, s), ((to >> 2) << 1) | (to & 1)]
        return remote(src, r.at[s, col], a2a_s.at[s, to], a2a_r.at[s, col], (row, to))

    def a2a_came(s, o):
        src = (col + o) & 15
        return remote(r.at[s, src], r.at[s, src], a2a_s.at[s, src], a2a_r.at[s, src], (row, src))

    def send_a2a(s):
        def go(o, _):
            a2a(s, o).start()
            return 0

        lax.fori_loop(1, 16, go, 0)
        r[s, col] = t[xl, (xl + 1 + (s >> 2)) & 1, order(z, s), z * 2 + core]

    def unpack_step(s):
        def wait(o, _):
            a2a_came(s, o).wait_recv()
            return 0

        lax.fori_loop(1, 16, wait, 0)
        hi, lo = halves(jnp.transpose(r[s].reshape(384, 128))[:96])
        block = jnp.dot(hi, unpack[...], preferred_element_type=F32)
        block += jnp.dot(lo, unpack[...], preferred_element_type=F32)
        amp[s >> 2, pl.ds(order(z, s) * 4, 4), row] = block.reshape(4, 24, 384)

    def pack_half(lanes, half):
        hi, lo = halves(x[lanes].reshape(512, 384))
        nt = (((1,), (1,)), ((), ()))
        rows = lax.dot_general(pack[half], hi, nt, preferred_element_type=F32)
        rows += lax.dot_general(pack[half], lo, nt, preferred_element_type=F32)
        for zz in range(4):
            t[lanes, half, zz] = rows[:, zz * 128 : (zz + 1) * 128].reshape(8, 24, 128)

    def slab(s, at, first=0, count=4):
        return amp.at[s >> 2, pl.ds(order(z, s) * 4 + first, count), at]

    far = (1 - xh) * 4 + y

    def x_send(s):
        return remote(slab(s, row), slab(s, row), x_s.at[s], x_r.at[s], other_xh)

    def x_came(s):
        return remote(slab(s, far), slab(s, far), x_s.at[s], x_r.at[s], other_xh)

    def y_row(way, which, steps):
        at_xh = 1 - xh if which else xh
        return at_xh * 4 + ((y + (4 - steps if way == 0 else steps)) & 3)

    def y_send(s, way, which):
        at = far if which else row
        return remote(slab(s, at), slab(s, at), y_s.at[s, way, which], y_r.at[s, way, which], ynext[way])

    def y_came(s, way, which):
        at = y_row(way, which, 1)
        return remote(slab(s, at), slab(s, at), y_s.at[s, way, which], y_r.at[s, way, which], ynext[way])

    def f_copy(s, way, which, steps):
        view = slab(s, y_row(way, which, steps), 2 * way, 2)
        return remote(view, view, f_s.at[s, way, which], f_r.at[s, way, which], ynext[way])

    def e_near(way, which):
        view = slab(EARLY, y_row(way, which, 1))
        return remote(view, view, e_s.at[0, way], e_r.at[0, way], other_xh)

    def e_far(way, which):
        view = slab(EARLY, y_row(way, which, 2), 2 * way, 2)
        return remote(view, view, e_s.at[1, way], e_r.at[1, way], other_xh)

    def compute(u):
        late = u >> 3
        n = (1 - late) * (u & 3) + late * (u >> 1)
        rh = (1 - late) * ((u >> 2) & 1) + late * (u & 1)
        h, zz, slot = n >> 2, order(z, n), n & 3

        @pl.when(u < 8)
        def _():
            def split_w(m, _):
                rows = pl.ds(pl.multiple_of(rh * 384 + m * 128, 128), 128)
                for c in range(2):
                    hi, lo = halves(wb[zz, c, rows, :])
                    whi[zz, rows, c * 384 : (c + 1) * 384] = hi
                    wlo[zz, rows, c * 384 : (c + 1) * 384] = lo
                return 0

            lax.fori_loop(0, 3, split_w, 0)

        @pl.when(rh == 0)
        def _():
            def split_a(k, _):
                hi, lo = halves(amp[h, zz * 4 + k].reshape(192, 384))
                rows = pl.ds(pl.multiple_of(k * 192, 64), 192)
                ahi[slot, rows, :] = hi
                alo[slot, rows, :] = lo
                return 0

            lax.fori_loop(0, 4, split_a, 0)

        rows = pl.ds(pl.multiple_of(rh * 384, 128), 384)
        a_hi = ahi[slot]
        w_hi = whi[zz, rows, :]
        total = jnp.dot(w_hi, a_hi, preferred_element_type=F32)
        total += jnp.dot(w_hi, alo[slot], preferred_element_type=F32)
        total += jnp.dot(wlo[zz, rows, :], a_hi, preferred_element_type=F32)
        acc[h, rows, :] += total

    def units(first, last):
        def go(u, _):
            compute(u)
            return 0

        lax.fori_loop(first, last, go, 0)

    def c_send(half):
        rows = pl.ds(half * 384, 384)
        return remote(acc.at[0, rows], part.at[rows], c_s.at[half], c_r.at[half], other_xl)

    acc[...] = jnp.zeros_like(acc)
    x[:, :, 96:, :] = jnp.zeros((2, 4, 32, 384), F32)
    loads[0].wait()
    for lanes in range(2):
        for quad in range(3):
            for kk in range(16):
                k = 8 * (kk // 4) + 4 * lanes + kk % 4
                at = kk % 4 * 24
                x[lanes, kk // 4, at : at + 24, quad * 128 : (quad + 1) * 128] = jnp.concatenate(
                    [d[k, quad * 4 + i] for i in range(4)], axis=-1
                )
    loads[1].wait()
    for half in range(2):
        pack_half(0, half)
        pack_half(1, half)
    pl.semaphore_wait(barrier, 18)

    for s in range(4):
        send_a2a(s)
    loads[2].wait()

    def own(s):
        unpack_step(s)
        x_send(s).start()
        for way in range(2):
            y_send(s, way, 0).start()

    def beyond(s):
        x_came(s).wait_recv()
        for way in range(2):
            y_send(s, way, 1).start()

    def f_wait(s):
        for way in range(2):
            f_copy(s, way, 0, 2).wait_recv()

        @pl.when(s != EARLY)
        def _():
            for way in range(2):
                f_copy(s, way, 1, 2).wait_recv()

        @pl.when(s == EARLY)
        def _():
            for way in range(2):
                e_far(way, 0).start()

    own(0)
    own(1)
    beyond(0)
    send_a2a(4)
    for way in range(2):
        w_own(way, 0).start()
    w_twin(0, 0, core, True).start()
    loads[3].wait()

    def body(s, _):
        for way in range(2):
            y_came(s, way, 0).wait_recv()
            f_copy(s, way, 0, 1).start()

        @pl.when((s < 7) & (s + 1 != EARLY))
        def _():
            beyond(s + 1)

        @pl.when(s != EARLY)
        def _():
            for way in range(2):
                y_came(s, way, 1).wait_recv()
                f_copy(s, way, 1, 1).start()

        @pl.when(s < 5)
        def _():
            own(s + 2)

        @pl.when(s == EARLY)
        def _():
            for way in range(2):
                e_near(way, 0).start()

        @pl.when(s == 1)
        def _():
            send_a2a(5)

        @pl.when(s == 2)
        def _():
            for way in range(2):
                w_came(way, 0).wait_recv()
                w_pass(way, 0, zfrom[way]).start()
            send_a2a(6)
            for way in range(2):
                w_own(way, 1 + way).start()
            send_a2a(7)
            for way in range(2):
                w_own(way, 2 - way).start()
            for off in (1, 3):
                w_twin(off, 0, core).start()
            w_twin(0, 0, 1 - core, True).wait_recv()

        @pl.when(s == 3)
        def _():
            for way in range(2):
                w_pass(way, 0, (z + 2) & 3).wait_recv()
            w_twin(2, 0, core).start()
            for off in (1, 3):
                w_twin(off, 0, 1 - core).wait_recv()

        @pl.when(s == 4)
        def _():
            for way in range(2):
                w_came(way, 1 + way).wait_recv()
                w_pass(way, 1, zfrom[way]).start()
            w_twin(2, 0, 1 - core).wait_recv()

        @pl.when(s == 5)
        def _():
            for way in range(2):
                w_came(way, 2 - way).wait_recv()
            for off in (1, 3):
                w_twin(off, 1, core).start()
            for off in (1, 3):
                w_twin(off, 1, 1 - core).wait_recv()

        @pl.when(s == 6)
        def _():
            w_twin(2, 1, 1 - core).wait_recv()

        @pl.when(s == EARLY + 2)
        def _():
            x_came(EARLY).wait_recv()
            for way in range(2):
                e_near(way, 1).wait_recv()
                e_far(way, 1).wait_recv()

        @pl.when((s >= 2) & (s <= 4))
        def _():
            units(s - 2, s - 1)

        @pl.when(s >= 5)
        def _():
            units(4 + (s - 5) * 3, jnp.minimum(7 + (s - 5) * 3, 12))

        @pl.when(s == 6)
        def _():
            c_send(1).start()

        @pl.when(s >= 1)
        def _():
            f_wait(s - 1)

        @pl.when(s == 4)
        def _():
            own(7)
            units(3, 4)
            c_send(0).start()

        @pl.when(s == 5)
        def _():
            for way in range(2):
                w_pass(way, 1, (z + 2) & 3).wait_recv()
            w_twin(2, 1, core).start()

        return 0

    lax.fori_loop(0, 8, body, 0)
    units(12, 14)

    def drain(s, _):
        def each(o, _):
            a2a(s, o).wait_send()
            return 0

        lax.fori_loop(1, 16, each, 0)
        x_send(s).wait_send()
        for way in range(2):
            y_send(s, way, 0).wait_send()

        @pl.when(s != EARLY)
        def _():
            for way in range(2):
                y_send(s, way, 1).wait_send()

        return 0

    lax.fori_loop(0, 8, drain, 0)
    for way in range(2):
        e_near(way, 0).wait_send()
        e_far(way, 0).wait_send()
        for p in range(3):
            w_own(way, p).wait_send()
        for half in range(2):
            w_pass(way, half, zfrom[way]).wait_send()
    w_twin(0, 0, core, True).wait_send()
    for off in (1, 2, 3):
        for half in range(2):
            w_twin(off, half, core).wait_send()

    def f_drain(s, _):
        for way in range(2):
            f_copy(s, way, 0, 1).wait_send()

        @pl.when(s != EARLY)
        def _():
            for way in range(2):
                f_copy(s, way, 1, 1).wait_send()

        return 0

    lax.fori_loop(0, 7, f_drain, 0)
    for half in range(2):
        c_send(half).wait_recv()
    acc[1] += part[...]
    f_wait(7)
    units(14, 16)
    out_ref[...] = acc[1]
    f_drain(7, 0)
    for half in range(2):
        c_send(half).wait_send()


def body(doubles, cycle_inter):
    pack, unpack = permutations()
    vmem, sems = pltpu.VMEM, pltpu.SemaphoreType.DMA
    return pl.pallas_call(
        kernel,
        out_shape=jax.ShapeDtypeStruct((768, 384), F32),
        in_specs=[pl.BlockSpec(memory_space=pl.ANY)] * 4,
        out_specs=pl.BlockSpec(memory_space=pltpu.VMEM),
        scratch_shapes=[
            vmem((32, 12, 24, 32), F32),
            vmem((2, 192, 384), BF16),
            vmem((384, 384), BF16),
            vmem((2, 4, 128, 384), F32),
            vmem((2, 2, 4, 8, 24, 128), F32),
            vmem((8, 16, 24, 128), F32),
            vmem((2, 16, 8, 24, 384), F32),
            vmem((4, 2, 768, 384), F32),
            vmem((4, 768, 768), BF16),
            vmem((4, 768, 768), BF16),
            vmem((4, 768, 384), BF16),
            vmem((4, 768, 384), BF16),
            vmem((2, 768, 384), F32),
            vmem((768, 384), F32),
            sems((4,)),
            sems((8, 16)), sems((8, 16)),
            sems((8,)), sems((8,)),
            sems((2, 2)), sems((2, 2)),
            sems((8, 2, 2)), sems((8, 2, 2)),
            sems((8, 2, 2)), sems((8, 2, 2)),
            sems((2, 3)), sems((2, 3)),
            sems((2, 2)), sems((2, 2)),
            sems((4, 2)), sems((4, 2)),
            sems((2,)), sems((2,)),
        ],
        compiler_params=pltpu.CompilerParams(
            collective_id=1, has_side_effects=True, vmem_limit_bytes=62 * 1024 * 1024
        ),
        name="cycle_term",
    )(
        jnp.transpose(doubles, (0, 3, 2, 1)),
        cycle_inter,
        jnp.asarray(pack, BF16),
        jnp.asarray(unpack, BF16),
    )


def solution(mesh):
    return jax.shard_map(
        body,
        mesh=mesh,
        in_specs=(P(None, None, "row", "col"), P("row", "col")),
        out_specs=P("row", "col"),
        check_vma=False,
    )
```

time: 110 us -> 105 us (0.955)
  Pallas kernels: 107 us -> 101 us
    pallas_call x1, Pallas kernels: 107 us -> 101 us  [body(): pl.pallas_call(kernel, out_shape=jax.ShapeDtypeStruct((768, 384), F32), i...]
where the time goes in v4:
time: 105 us; the launch traced here: 104 us
  Pallas kernels  101 us (96%)
  local copies, waits for them, and re-layouts  2.36 us (2%)
    pallas_call x1, Pallas kernels, body(): pl.pallas_call(kernel, out_shape=jax.ShapeDtypeStruct((768, 384), F32), i...  101 us
    unnamed x1, local copies, waits for them, and re-layouts  2.36 us

profile of v4, /device:TPU:2, one launch (start us, length us, event | category | flops | bytes accessed | tf_op | source)
XLA Modules:
  0.0 103.8 jit_solution(5532284440242154574)
XLA Ops:
  0.0 101.5 %cycle_term.1 = f32[768,384]{1,0:T(8,128)} custom-call(f32[32,12,24,32]{3,2,1,0:T(8,128)} %bitcast.1, f32[768,384]{1,0:T(8,128)} %w_hbm.1, bf16[2,192,384]{2,1,0:T(8,128)(2,1)} %constant.4.clone.pack_hbm, bf16[384,384]{1,0:T(8,128)(2,1)} %constant.5.clone.unpack_hbm), custom_call_target="tpu_custom_call" | custom-call | tf_op jit(solution)/shard_map/cycle_term/pallas_call | solution.py:448
  101.5 2.4 %copy.6 = f32[768,384]{1,0:T(8,128)} copy(f32[768,384]{1,0:T(8,128)} %cycle_term.1) | data formatting | bytes 2359296

commit v5 on v4

--- a/solution.py
+++ b/solution.py
@@ -435,8 +435,14 @@
         c_send(half).wait_recv()
     acc[1] += part[...]
     f_wait(7)
-    units(14, 16)
-    out_ref[...] = acc[1]
+    outs = []
+    for half in range(2):
+        units(14 + half, 15 + half)
+        rows = pl.ds(half * 384, 384)
+        outs.append(pltpu.make_async_copy(acc.at[1, rows], out_ref.at[rows], in_sem.at[half]))
+        outs[-1].start()
+    for copy in outs:
+        copy.wait()
     f_drain(7, 0)
     for half in range(2):
         c_send(half).wait_send()
@@ -449,7 +455,7 @@
         kernel,
         out_shape=jax.ShapeDtypeStruct((768, 384), F32),
         in_specs=[pl.BlockSpec(memory_space=pl.ANY)] * 4,
-        out_specs=pl.BlockSpec(memory_space=pltpu.VMEM),
+        out_specs=pl.BlockSpec(memory_space=pl.ANY),
         scratch_shapes=[
             vmem((32, 12, 24, 32), F32),
             vmem((2, 192, 384), BF16),
@@ -477,7 +483,7 @@
             sems((2,)), sems((2,)),
         ],
         compiler_params=pltpu.CompilerParams(
-            collective_id=1, has_side_effects=True, vmem_limit_bytes=62 * 1024 * 1024
+            collective_id=1, has_side_effects=True, vmem_limit_bytes=64000000
         ),
         name="cycle_term",
     )(

time: 105 us -> 104 us (level)
  no operation moved by 1% of the time
where the time goes in v5:
time: 104 us; the launch traced here: 103 us
  Pallas kernels  101 us (97%)
  local copies, waits for them, and re-layouts  2.36 us (2%)
    pallas_call x1, Pallas kernels, body(): pl.pallas_call(kernel, out_shape=jax.ShapeDtypeStruct((768, 384), F32), i...  101 us
    unnamed x1, local copies, waits for them, and re-layouts  2.36 us

profile of v5, /device:TPU:2, one launch (start us, length us, event | category | flops | bytes accessed | tf_op | source)
XLA Modules:
  0.0 103.5 jit_solution(15722201640267608950)
XLA Ops:
  0.0 101.1 %cycle_term.1 = f32[768,384]{1,0:T(8,128)} custom-call(f32[32,12,24,32]{3,2,1,0:T(8,128)} %bitcast.1, f32[768,384]{1,0:T(8,128)} %w_hbm.1, bf16[2,192,384]{2,1,0:T(8,128)(2,1)} %constant.4.clone.pack_hbm, bf16[384,384]{1,0:T(8,128)(2,1)} %constant.5.clone.unpack_hbm), custom_call_target="tpu_custom_call" | custom-call | tf_op jit(solution)/shard_map/cycle_term/pallas_call | solution.py:454
  101.1 2.4 %copy.6 = f32[768,384]{1,0:T(8,128)} copy(f32[768,384]{1,0:T(8,128)} %cycle_term.1) | data formatting | bytes 2359296
